TPU v7x, 32 devices: a whole 2x2x4 slice. The times are simulated.
32 devices in a mesh: dp: 8 (over y, x, core), fsdp: 4 (over z).
Axes of the slice: x: 2, y: 2, z: 4, core: 2. Of those that a mesh axis runs over, the one named last changes fastest.
Arguments:
- gene_ids: int32 [32, 2048], P(('dp', 'fsdp')), may hold values from 0 to 12799
- expr_bins: int32 [32, 2048], P(('dp', 'fsdp')), may hold values from 0 to 63
- study_ids: int32 [32], P(('dp', 'fsdp')), may hold values from 0 to 63
- lengths: int32 [32], P(('dp', 'fsdp')), may hold values from 256 to 2048, as said below
- prior_embed: bfloat16 [32, 2048, 256], P(('dp', 'fsdp')), may hold values from -3 to 3
- cotangent: bfloat16 [32, 2048, 256], P(('dp', 'fsdp')), may hold values from -6 to 6
- gene_table: bfloat16 [12800, 256], P('fsdp'), may hold values from -3 to 3
- expr_table: bfloat16 [64, 256], P('fsdp'), may hold values from -3 to 3
- study_table: bfloat16 [64, 256], P('fsdp'), may hold values from -3 to 3
- position_table: bfloat16 [2048, 256], P('fsdp'), may hold values from -3 to 3
- norm1_gain: bfloat16 [256], P('fsdp'), may hold values from 0.099609375 to 1.8984375
- norm1_shift: bfloat16 [256], P('fsdp'), may hold values from -1.5 to 1.5
- w_qkv: bfloat16 [256, 768], P('fsdp'), may hold values from -0.375 to 0.375
- bias_query: bfloat16 [256], P('fsdp'), may hold values from -1.5 to 1.5
- bias_value: bfloat16 [256], P('fsdp'), may hold values from -1.5 to 1.5
- w_output: bfloat16 [256, 256], P('fsdp'), may hold values from -6 to 6
- bias_output: bfloat16 [256], P('fsdp'), may hold values from -1.5 to 1.5
- norm2_gain: bfloat16 [256], P('fsdp'), may hold values from 0.099609375 to 1.8984375
- norm2_shift: bfloat16 [256], P('fsdp'), may hold values from -1.5 to 1.5
- w_up_proj: bfloat16 [256, 512], P('fsdp'), may hold values from -0.375 to 0.375
- bias_up: bfloat16 [512], P('fsdp'), may hold values from -1.5 to 1.5
- w_down_proj: bfloat16 [512, 256], P('fsdp'), may hold values from -0.25 to 0.25
- bias_down: bfloat16 [256], P('fsdp'), may hold values from -1.5 to 1.5
Outputs:
- hidden_out: bfloat16 [32, 2048, 256], P(('dp', 'fsdp'))
- grad_gene_table: float32 [12800, 256], P('fsdp')
- update_count: int32 [12800], P('fsdp')
- grad_expr_table: float32 [64, 256], P('fsdp')
- grad_study_table: float32 [64, 256], P('fsdp')
- grad_position_table: float32 [2048, 256], P('fsdp')
- grad_norm1_gain: float32 [256], P('fsdp')
- grad_norm1_shift: float32 [256], P('fsdp')
- grad_w_qkv: float32 [256, 768], P('fsdp')
- grad_bias_query: float32 [256], P('fsdp')
- grad_bias_value: float32 [256], P('fsdp')
- grad_w_output: float32 [256, 256], P('fsdp')
- grad_bias_output: float32 [256], P('fsdp')
- grad_norm2_gain: float32 [256], P('fsdp')
- grad_norm2_shift: float32 [256], P('fsdp')
- grad_w_up_proj: float32 [256, 512], P('fsdp')
- grad_bias_up: float32 [512], P('fsdp')
- grad_w_down_proj: float32 [512, 256], P('fsdp')
- grad_bias_down: float32 [256], P('fsdp')
Inputs may be any that keep to these rules, and one draw needn't show every extreme that they name: Slots from lengths[c] on are padding; some cell has 2048 genes and some 2048 // 8.
All inputs are finite; a program needn't handle non-finite values.
Results may differ from a plain program's by a relative error of at most 0.0082.
Values may be sent and summed in bfloat16 or wider, within the bound.
No kernel may reach another device: no remote copies, remote signals or barrier semaphores. Data moves between devices by JAX's collectives and lax.ppermute only.
A program may use at most 128 MiB of HBM per device.

v0:
```python
import jax
import jax.numpy as jnp
from jax import lax
from jax.sharding import PartitionSpec as P

HEADS = 4
epsilon = 1e-05
highest = lax.Precision.HIGHEST


def normalize(values):
    average = jnp.mean(values, axis=-1, keepdims=True)
    centered = values - average
    variance = jnp.mean(centered * centered, axis=-1, keepdims=True)
    return centered * lax.rsqrt(variance + epsilon)


def norm_back(values, gain, grad):
    unused, pullback = jax.vjp(lambda entries, scale: normalize(entries) * scale, values, gain)
    grad_rows, grad_gain = pullback(grad)
    return (grad_rows, grad_gain, jnp.sum(grad, axis=0))


def matmul(left, right):
    return jnp.dot(left, right, preferred_element_type=jnp.float32)


def weight_grad(left, right):
    return lax.dot_general(
        left, right, (((0,), (0,)), ((), ())), preferred_element_type=jnp.float32
    )


def back_matmul(left, right):
    return lax.dot_general(
        left, right, (((1,), (1,)), ((), ())), preferred_element_type=jnp.float32
    )


def table_grad(hits, grads):
    return lax.dot_general(
        hits, grads, (((0,), (0,)), ((), ())), precision=highest, preferred_element_type=jnp.float32
    )


def attend(query, keys, values, key_mask, block):
    length, heads, head_size = query.shape
    scale = head_size ** (-0.5)
    query_blocks = query.reshape(length // block, block, heads, head_size)

    def one_block(query_block):
        scores = (
            jnp.einsum("qhk,shk->hqs", query_block, keys, preferred_element_type=jnp.float32)
            * scale
        )
        scores = jnp.where(key_mask[None, None, :] > 0, scores, -1000000000.0)
        peak = jnp.max(scores, axis=-1, keepdims=True)
        raised = jnp.exp(scores - peak)
        total = jnp.sum(raised, axis=-1, keepdims=True)
        probs = (raised / total).astype(jnp.bfloat16)
        attended = jnp.einsum("hqs,shk->qhk", probs, values, preferred_element_type=jnp.float32)
        return (attended.astype(jnp.bfloat16), (peak + jnp.log(total))[..., 0])

    attended, log_total = lax.map(one_block, query_blocks)
    return (attended.reshape(length, heads, head_size), log_total)


def attend_back(query, keys, values, key_mask, log_total, grad_attended, block):
    length, heads, head_size = query.shape
    scale = head_size ** (-0.5)
    query_blocks = query.reshape(length // block, block, heads, head_size)
    grad_blocks = grad_attended.reshape(length // block, block, heads, head_size)

    def one_block(carry, embedding_parts):
        grad_keys, grad_values = carry
        query_block, grad_block, log_block = embedding_parts
        scores = (
            jnp.einsum("qhk,shk->hqs", query_block, keys, preferred_element_type=jnp.float32)
            * scale
        )
        scores = jnp.where(key_mask[None, None, :] > 0, scores, -1000000000.0)
        probs = jnp.exp(scores - log_block[..., None])
        probs_low = probs.astype(jnp.bfloat16)
        grad_probs = jnp.einsum(
            "qhk,shk->hqs", grad_block, values, preferred_element_type=jnp.float32
        )
        inner = jnp.sum(probs * grad_probs, axis=-1, keepdims=True)
        grad_scores = (probs * (grad_probs - inner)).astype(jnp.bfloat16)
        grad_query = (
            jnp.einsum("hqs,shk->qhk", grad_scores, keys, preferred_element_type=jnp.float32)
            * scale
        )
        grad_keys = (
            grad_keys
            + jnp.einsum(
                "hqs,qhk->shk", grad_scores, query_block, preferred_element_type=jnp.float32
            )
            * scale
        )
        grad_values = grad_values + jnp.einsum(
            "hqs,qhk->shk", probs_low, grad_block, preferred_element_type=jnp.float32
        )
        return ((grad_keys, grad_values), grad_query)

    starting = jnp.zeros((length, heads, head_size), jnp.float32)
    (grad_keys, grad_values), grad_query = lax.scan(
        one_block, (starting, starting), (query_blocks, grad_blocks, log_total)
    )
    return (grad_query.reshape(length, heads, head_size), grad_keys, grad_values)


def body(
    gene_ids,
    expr_bins,
    study_ids,
    lengths,
    prior_embed,
    cotangent,
    gene_table,
    expr_table,
    study_table,
    position_table,
    norm1_gain,
    norm1_shift,
    w_qkv,
    bias_query,
    bias_value,
    w_output,
    bias_output,
    norm2_gain,
    norm2_shift,
    w_up_proj,
    bias_up,
    w_down_proj,
    bias_down,
):
    (
        full_gene,
        full_expr,
        full_study,
        full_position,
        gain_one,
        shift_one,
        full_qkv,
        query_bias,
        value_bias,
        full_output,
        output_bias,
        gain_two,
        shift_two,
        full_up,
        up_bias,
        full_down,
        down_bias,
    ) = (
        lax.all_gather(gene_table, "fsdp", axis=0, tiled=True),
        lax.all_gather(expr_table, "fsdp", axis=0, tiled=True),
        lax.all_gather(study_table, "fsdp", axis=0, tiled=True),
        lax.all_gather(position_table, "fsdp", axis=0, tiled=True),
        lax.all_gather(norm1_gain, "fsdp", axis=0, tiled=True),
        lax.all_gather(norm1_shift, "fsdp", axis=0, tiled=True),
        lax.all_gather(w_qkv, "fsdp", axis=0, tiled=True),
        lax.all_gather(bias_query, "fsdp", axis=0, tiled=True),
        lax.all_gather(bias_value, "fsdp", axis=0, tiled=True),
        lax.all_gather(w_output, "fsdp", axis=0, tiled=True),
        lax.all_gather(bias_output, "fsdp", axis=0, tiled=True),
        lax.all_gather(norm2_gain, "fsdp", axis=0, tiled=True),
        lax.all_gather(norm2_shift, "fsdp", axis=0, tiled=True),
        lax.all_gather(w_up_proj, "fsdp", axis=0, tiled=True),
        lax.all_gather(bias_up, "fsdp", axis=0, tiled=True),
        lax.all_gather(w_down_proj, "fsdp", axis=0, tiled=True),
        lax.all_gather(bias_down, "fsdp", axis=0, tiled=True),
    )
    cells, length = gene_ids.shape
    width = full_gene.shape[1]
    rows = cells * length
    heads = HEADS
    head_size = width // heads
    block = min(512, length)

    def shaped(array):
        return array.reshape(cells, length, heads, head_size)

    key_mask = (lax.broadcasted_iota(jnp.int32, (cells, length), 1) < lengths[:, None]).astype(
        jnp.float32
    )
    flat_mask = key_mask.reshape(rows, 1)
    embedded = (
        full_gene[gene_ids].astype(jnp.float32)
        + full_expr[expr_bins].astype(jnp.float32)
        + full_study[study_ids].astype(jnp.float32)[:, None, :]
        + full_position.astype(jnp.float32)[None]
        + prior_embed.astype(jnp.float32)
    )
    inputs = (embedded * key_mask[..., None]).reshape(rows, width)
    normed_one = (
        normalize(inputs) * gain_one.astype(jnp.float32) + shift_one.astype(jnp.float32)
    ).astype(jnp.bfloat16)
    mixed = matmul(normed_one, full_qkv)
    query = (mixed[:, :width] + query_bias.astype(jnp.float32)).astype(jnp.bfloat16)
    keys = mixed[:, width : 2 * width].astype(jnp.bfloat16)
    values = (mixed[:, 2 * width :] + value_bias.astype(jnp.float32)).astype(jnp.bfloat16)
    attended, log_total = lax.map(
        lambda embedding_parts: attend(
            embedding_parts[0], embedding_parts[1], embedding_parts[2], embedding_parts[3], block
        ),
        (shaped(query), shaped(keys), shaped(values), key_mask),
    )
    attended = attended.reshape(rows, width)
    branch = matmul(attended, full_output) + output_bias.astype(jnp.float32)
    middle = inputs + branch
    normed_two = (
        normalize(middle) * gain_two.astype(jnp.float32) + shift_two.astype(jnp.float32)
    ).astype(jnp.bfloat16)
    upward = matmul(normed_two, full_up) + up_bias.astype(jnp.float32)
    activated = jax.nn.gelu(upward, approximate=False).astype(jnp.bfloat16)
    result = (middle + (matmul(activated, full_down) + down_bias.astype(jnp.float32))) * flat_mask
    hidden_out = result.astype(jnp.bfloat16).reshape(cells, length, width)
    back_gain_one, back_qkv, back_output, back_gain_two, back_up, back_down = (
        lax.all_gather(norm1_gain, "fsdp", axis=0, tiled=True),
        lax.all_gather(w_qkv, "fsdp", axis=0, tiled=True),
        lax.all_gather(w_output, "fsdp", axis=0, tiled=True),
        lax.all_gather(norm2_gain, "fsdp", axis=0, tiled=True),
        lax.all_gather(w_up_proj, "fsdp", axis=0, tiled=True),
        lax.all_gather(w_down_proj, "fsdp", axis=0, tiled=True),
    )
    grad_result = cotangent.astype(jnp.float32).reshape(rows, width) * flat_mask
    grad_low = grad_result.astype(jnp.bfloat16)
    grad_down_w = weight_grad(activated, grad_low)
    grad_down_b = jnp.sum(grad_result, axis=0)
    grad_activated = back_matmul(grad_low, back_down)
    unused, gelu_pull = jax.vjp(lambda entries: jax.nn.gelu(entries, approximate=False), upward)
    grad_upward = gelu_pull(grad_activated)[0].astype(jnp.bfloat16)
    grad_up_w = weight_grad(normed_two, grad_upward)
    grad_up_b = jnp.sum(grad_upward.astype(jnp.float32), axis=0)
    grad_normed_two = back_matmul(grad_upward, back_up)
    grad_mid_norm, grad_gain_two, grad_shift_two = norm_back(
        middle, back_gain_two.astype(jnp.float32), grad_normed_two
    )
    grad_middle = grad_result + grad_mid_norm
    grad_branch = grad_middle.astype(jnp.bfloat16)
    grad_output_w = weight_grad(attended, grad_branch)
    grad_output_b = jnp.sum(grad_branch.astype(jnp.float32), axis=0)
    grad_attended = back_matmul(grad_branch, back_output).astype(jnp.bfloat16)
    grad_query, grad_keys, grad_values = lax.map(
        lambda embedding_parts: attend_back(
            embedding_parts[0],
            embedding_parts[1],
            embedding_parts[2],
            embedding_parts[3],
            embedding_parts[4],
            embedding_parts[5],
            block,
        ),
        (shaped(query), shaped(keys), shaped(values), key_mask, log_total, shaped(grad_attended)),
    )
    grad_query = grad_query.reshape(rows, width).astype(jnp.bfloat16)
    grad_keys = grad_keys.reshape(rows, width).astype(jnp.bfloat16)
    grad_values = grad_values.reshape(rows, width).astype(jnp.bfloat16)
    grad_mixed = jnp.concatenate([grad_query, grad_keys, grad_values], axis=1)
    grad_qkv_w = weight_grad(normed_one, grad_mixed)
    grad_query_b = jnp.sum(grad_query.astype(jnp.float32), axis=0)
    grad_value_b = jnp.sum(grad_values.astype(jnp.float32), axis=0)
    grad_normed_one = back_matmul(grad_mixed, back_qkv)
    grad_in_norm, grad_gain_one, grad_shift_one = norm_back(
        inputs, back_gain_one.astype(jnp.float32), grad_normed_one
    )
    grad_inputs = (grad_middle + grad_in_norm) * flat_mask
    grad_cells = grad_inputs.reshape(cells, length, width)
    bin_hits = (
        expr_bins.reshape(rows, 1) == lax.broadcasted_iota(jnp.int32, (1, full_expr.shape[0]), 1)
    ).astype(jnp.float32)
    grad_expr = table_grad(bin_hits, grad_inputs)
    study_hits = (
        study_ids[:, None] == lax.broadcasted_iota(jnp.int32, (1, full_study.shape[0]), 1)
    ).astype(jnp.float32)
    grad_study = table_grad(study_hits, jnp.sum(grad_cells, axis=1))
    grad_position = jnp.sum(grad_cells, axis=0)
    flat_ids = gene_ids.reshape(rows)
    vocab = full_gene.shape[0]
    dense_grad = jnp.zeros((vocab, width), jnp.float32).at[flat_ids].add(grad_inputs)
    dense_count = jnp.zeros((vocab,), jnp.float32).at[flat_ids].add(flat_mask[:, 0])
    (
        table_share,
        count_share,
        expr_share,
        study_share,
        position_share,
        gain_one_share,
        shift_one_share,
        qkv_share,
        query_b_share,
        value_b_share,
        output_share,
        output_b_share,
        gain_two_share,
        shift_two_share,
        up_share,
        up_b_share,
        down_share,
        down_b_share,
    ) = (
        lax.psum_scatter(dense_grad, "fsdp", scatter_dimension=0, tiled=True),
        lax.psum_scatter(dense_count, "fsdp", scatter_dimension=0, tiled=True),
        lax.psum_scatter(grad_expr, "fsdp", scatter_dimension=0, tiled=True),
        lax.psum_scatter(grad_study, "fsdp", scatter_dimension=0, tiled=True),
        lax.psum_scatter(grad_position, "fsdp", scatter_dimension=0, tiled=True),
        lax.psum_scatter(grad_gain_one, "fsdp", scatter_dimension=0, tiled=True),
        lax.psum_scatter(grad_shift_one, "fsdp", scatter_dimension=0, tiled=True),
        lax.psum_scatter(grad_qkv_w, "fsdp", scatter_dimension=0, tiled=True),
        lax.psum_scatter(grad_query_b, "fsdp", scatter_dimension=0, tiled=True),
        lax.psum_scatter(grad_value_b, "fsdp", scatter_dimension=0, tiled=True),
        lax.psum_scatter(grad_output_w, "fsdp", scatter_dimension=0, tiled=True),
        lax.psum_scatter(grad_output_b, "fsdp", scatter_dimension=0, tiled=True),
        lax.psum_scatter(grad_gain_two, "fsdp", scatter_dimension=0, tiled=True),
        lax.psum_scatter(grad_shift_two, "fsdp", scatter_dimension=0, tiled=True),
        lax.psum_scatter(grad_up_w, "fsdp", scatter_dimension=0, tiled=True),
        lax.psum_scatter(grad_up_b, "fsdp", scatter_dimension=0, tiled=True),
        lax.psum_scatter(grad_down_w, "fsdp", scatter_dimension=0, tiled=True),
        lax.psum_scatter(grad_down_b, "fsdp", scatter_dimension=0, tiled=True),
    )
    (
        table_sum,
        count_sum,
        expr_sum,
        study_sum,
        position_sum,
        gain_one_sum,
        shift_one_sum,
        qkv_sum,
        query_b_sum,
        value_b_sum,
        output_sum,
        output_b_sum,
        gain_two_sum,
        shift_two_sum,
        up_sum,
        up_b_sum,
        down_sum,
        down_b_sum,
    ) = lax.psum(
        (
            table_share,
            count_share,
            expr_share,
            study_share,
            position_share,
            gain_one_share,
            shift_one_share,
            qkv_share,
            query_b_share,
            value_b_share,
            output_share,
            output_b_share,
            gain_two_share,
            shift_two_share,
            up_share,
            up_b_share,
            down_share,
            down_b_share,
        ),
        "dp",
    )
    return (
        hidden_out,
        table_sum,
        count_sum.astype(jnp.int32),
        expr_sum,
        study_sum,
        position_sum,
        gain_one_sum,
        shift_one_sum,
        qkv_sum,
        query_b_sum,
        value_b_sum,
        output_sum,
        output_b_sum,
        gain_two_sum,
        shift_two_sum,
        up_sum,
        up_b_sum,
        down_sum,
        down_b_sum,
    )


def solution(mesh):
    return jax.shard_map(
        body,
        mesh=mesh,
        in_specs=(
            P(("dp", "fsdp"), None),
            P(("dp", "fsdp"), None),
            P(("dp", "fsdp")),
            P(("dp", "fsdp")),
            P(("dp", "fsdp"), None, None),
            P(("dp", "fsdp"), None, None),
            P("fsdp", None),
            P("fsdp", None),
            P("fsdp", None),
            P("fsdp", None),
            P("fsdp"),
            P("fsdp"),
            P("fsdp", None),
            P("fsdp"),
            P("fsdp"),
            P("fsdp", None),
            P("fsdp"),
            P("fsdp"),
            P("fsdp"),
            P("fsdp", None),
            P("fsdp"),
            P("fsdp", None),
            P("fsdp"),
        ),
        out_specs=(
            P(("dp", "fsdp"), None, None),
            P("fsdp", None),
            P("fsdp"),
            P("fsdp", None),
            P("fsdp", None),
            P("fsdp", None),
            P("fsdp"),
            P("fsdp"),
            P("fsdp", None),
            P("fsdp"),
            P("fsdp"),
            P("fsdp", None),
            P("fsdp"),
            P("fsdp"),
            P("fsdp"),
            P("fsdp", None),
            P("fsdp"),
            P("fsdp", None),
            P("fsdp"),
        ),
        check_vma=False,
    )
```

profile of v0, /device:TPU:0, one launch (start us, length us, event | category | flops | bytes accessed | tf_op | source)
XLA Modules:
  0.0 905.6 jit_solution(10123542352486221909)
XLA Ops:
  20.7 16.2 %all-reduce.21 = (bf16[256]{0:T(256)(128)(2,1)S(1)}, bf16[256]{0:T(256)(128)(2,1)S(1)}, bf16[256]{0:T(256)(128)(2,1)S(1)}, bf16[256]{0:T(256)(128)(2,1)S(1)}, bf...) all-reduce(bf16[256]{0:T(256)(128)(2,1)S(1)} %dynamic-update-slice., ...), channel_id=1, replica_groups=mesh['dp'=8,'fsdp'=4] {'fsdp'}, use_global_device_ids=true, to_apply=%add.1 | all-reduce | flops 2048 | bytes 8192
  40.7 7.9 all-gather
  49.2 16.0 %all_gather.58 = bf16[64,256]{1,0:T(8,128)(2,1)S(1)} all-gather(bf16[16,256]{1,0:T(8,128)(2,1)} %param.34), channel_id=1, replica_groups=mesh['dp'=8,'fsdp'=4] {'fsdp'}, dimensions={0}, use_global_device_ids=true | all-gather | bytes 40960 | tf_op jit(solution)/shard_map/all_gather | solution.py:157
  65.2 7.5 gather_fusion.1
  76.3 15.8 %all_gather.59 = bf16[64,256]{1,0:T(8,128)(2,1)S(1)} all-gather(bf16[16,256]{1,0:T(8,128)(2,1)S(1)} %copy-done.55), channel_id=1, replica_groups=mesh['dp'=8,'fsdp'=4] {'fsdp'}, dimensions={0}, use_global_device_ids=true | all-gather | bytes 40960 | tf_op jit(solution)/shard_map/all_gather | solution.py:158
  92.2 18.9 %all_gather.66 = bf16[256,256]{1,0:T(8,128)(2,1)} all-gather(bf16[64,256]{1,0:T(8,128)(2,1)S(1)} %copy-done.49), channel_id=1, replica_groups=mesh['dp'=8,'fsdp'=4] {'fsdp'}, dimensions={0}, use_global_device_ids=true | all-gather | bytes 163840 | tf_op jit(solution)/shard_map/all_gather | solution.py:165
  111.1 22.1 %all_gather.70 = bf16[256,512]{1,0:T(8,128)(2,1)} all-gather(bf16[64,512]{1,0:T(8,128)(2,1)S(1)} %copy-done.44), channel_id=1, replica_groups=mesh['dp'=8,'fsdp'=4] {'fsdp'}, dimensions={0}, use_global_device_ids=true | all-gather | bytes 327680 | tf_op jit(solution)/shard_map/all_gather | solution.py:169
  133.2 16.9 %all_gather.72 = bf16[512,256]{1,0:T(8,128)(2,1)} all-gather(bf16[128,256]{1,0:T(8,128)(2,1)S(1)} %copy-done.45), channel_id=1, replica_groups=mesh['dp'=8,'fsdp'=4] {'fsdp'}, dimensions={0}, use_global_device_ids=true | all-gather | bytes 327680 | tf_op jit(solution)/shard_map/all_gather | solution.py:171
  150.7 17.1 %all_gather.63 = bf16[256,768]{1,0:T(8,128)(2,1)S(1)} all-gather(bf16[64,768]{1,0:T(8,128)(2,1)} %param.39), channel_id=1, replica_groups=mesh['dp'=8,'fsdp'=4] {'fsdp'}, dimensions={0}, use_global_device_ids=true | all-gather | bytes 491520 | tf_op jit(solution)/shard_map/all_gather | solution.py:162
  167.8 12.3 %gather_fusion = bf16[2048,256]{1,0:T(8,128)(2,1)} fusion(bf16[12800,256]{1,0:T(8,128)(2,1)} %all-gather.4.cloned.1.call-done, s32[2048]{0:T(1024)S(1)} %broadcast_clamp_fusion.1), kind=kCustom, calls=%fused_computation | custom fusion | bytes 2105344 | tf_op jit(solution)/shard_map/gather | solution.py:189
  191.9 53.9 %while.49 = (s32[]{:T(128)}, bf16[4,512,4,64]{1,3,2,0:T(8,128)(2,1)}, f32[4,4,512]{2,1,0:T(4,128)S(1)}, bf16[4,512,4,64]{1,3,2,0:T(8,128)(2,1)}, bf16[2048,4,64]...) while((s32[]{:T(128)}, bf16[4,512,4,64]{1,3,2,0:T(8,128)(2,1)}, ...), condition=%wide.region_5.6_spmd.clone, body=%wide.region_2.5_spmd.clone.sunk | while | flops 1124208640 | bytes 53026924 | solution.py:64
  249.5 10.9 %multiply_convert_fusion.1 = (bf16[2048,512]{1,0:T(8,128)(2,1)}, f32[2048,512]{1,0:T(8,128)S(1)}, f32[2048,512]{1,0:T(8,128)S(1)}) fusion(f32[512]{0:T(512)S(1)} %bitcast.190, bf16[256,512]{1,0:T(8,128)(2,1)S(1)} %copy-done.26, f32[2048,256]{0,1:T(8,128)S(1)} %get-tuple-element.435, f32[256]{0:T(256)S(1)} %copy-done.72, f32[256]{0:T(256)S(1)} %copy-done.64, ...), kind=kOutput, calls=%fused_computation.63 | convolution fusion | flops 608698368 | bytes 12865536 | tf_op jit(solution)/shard_map/dot_general | solution.py:25
  297.0 166.8 %while.50 = (s32[]{:T(128)}, f32[2048,4,64]{0,2,1:T(8,128)}, f32[2048,4,64]{0,2,1:T(8,128)}, bf16[4,512,4,64]{1,3,2,0:T(8,128)(2,1)}, bf16[4,512,4,64]{1,3,2,0:T...) while((s32[]{:T(128)}, f32[2048,4,64]{0,2,1:T(8,128)}, ...), condition=%wide.region_12.13_spmd.clone, body=%wide.region_10.12_spmd.clone.sunk | while | flops 2750025728 | bytes 172556464 | solution.py:106
  306.8 9.5 %multiply_reduce_fusion.8 = (f32[4,512]{1,0:T(4,128)S(1)}, f32[4,512,2048]{2,1,0:T(8,128)}) fusion(f32[4,512,2048]{2,1,0:T(8,128)S(1)} %fusion.154, f32[4,512]{1,0:T(4,128)S(1)} %dynamic-slice_bitcast_fusion.2, pred[2048]{0:T(1024)(128)(4,1)S(1)} %convert_compare_fusion.5, bf16[2048,4,64]{0,2,1:T(8,128)(2,1)S(1)} %get-tuple-element.611, ...), kind=kOutput, calls=%fused_computation.25.clone.1 | convolution fusion | flops 557840384 | bytes 34883588 | tf_op jit(solution)/shard_map/while/body/eval_jaxpr/while/body/eval_jaxpr/qhk,shk->hqs/dot_general | solution.py:84
  316.4 10.8 %multiply_convert_fusion.3 = bf16[4,512,2048]{2,1,0:T(8,128)(2,1)} fusion(f32[4,512,2048]{2,1,0:T(8,128)} %get-tuple-element.553, f32[4,512,2048]{2,1,0:T(8,128)S(1)} %fusion.154, f32[4,512]{1,0:T(4,128)S(1)} %get-tuple-element.554, f32[4,512]{1,0:T(4,128)S(1)} %dynamic-slice_bitcast_fusion.2, pred[2048]{0:T(1024)(128)(4,1)S(1)} %convert_compare_fusion.5), kind=kLoop, calls=%fused_computation.24.clone.1 | loop fusion | flops 25165824 | bytes 41961472 | tf_op jit(solution)/shard_map/while/body/eval_jaxpr/while/body/eval_jaxpr/convert_element_type | solution.py:88
  327.1 6.9 fusion.157
  348.1 9.5 %multiply_reduce_fusion.8 = (f32[4,512]{1,0:T(4,128)S(1)}, f32[4,512,2048]{2,1,0:T(8,128)}) fusion(f32[4,512,2048]{2,1,0:T(8,128)S(1)} %fusion.154, f32[4,512]{1,0:T(4,128)S(1)} %dynamic-slice_bitcast_fusion.2, pred[2048]{0:T(1024)(128)(4,1)S(1)} %convert_compare_fusion.5, bf16[2048,4,64]{0,2,1:T(8,128)(2,1)S(1)} %get-tuple-element.611, ...), kind=kOutput, calls=%fused_computation.25.clone.1 | convolution fusion | flops 557840384 | bytes 34883588 | tf_op jit(solution)/shard_map/while/body/eval_jaxpr/while/body/eval_jaxpr/qhk,shk->hqs/dot_general | solution.py:84
  357.7 10.7 %multiply_convert_fusion.3 = bf16[4,512,2048]{2,1,0:T(8,128)(2,1)} fusion(f32[4,512,2048]{2,1,0:T(8,128)} %get-tuple-element.553, f32[4,512,2048]{2,1,0:T(8,128)S(1)} %fusion.154, f32[4,512]{1,0:T(4,128)S(1)} %get-tuple-element.554, f32[4,512]{1,0:T(4,128)S(1)} %dynamic-slice_bitcast_fusion.2, pred[2048]{0:T(1024)(128)(4,1)S(1)} %convert_compare_fusion.5), kind=kLoop, calls=%fused_computation.24.clone.1 | loop fusion | flops 25165824 | bytes 41961472 | tf_op jit(solution)/shard_map/while/body/eval_jaxpr/while/body/eval_jaxpr/convert_element_type | solution.py:88
  368.3 6.9 fusion.157
  390.0 9.5 %multiply_reduce_fusion.8 = (f32[4,512]{1,0:T(4,128)S(1)}, f32[4,512,2048]{2,1,0:T(8,128)}) fusion(f32[4,512,2048]{2,1,0:T(8,128)S(1)} %fusion.154, f32[4,512]{1,0:T(4,128)S(1)} %dynamic-slice_bitcast_fusion.2, pred[2048]{0:T(1024)(128)(4,1)S(1)} %convert_compare_fusion.5, bf16[2048,4,64]{0,2,1:T(8,128)(2,1)S(1)} %get-tuple-element.611, ...), kind=kOutput, calls=%fused_computation.25.clone.1 | convolution fusion | flops 557840384 | bytes 34883588 | tf_op jit(solution)/shard_map/while/body/eval_jaxpr/while/body/eval_jaxpr/qhk,shk->hqs/dot_general | solution.py:84
  399.5 10.7 %multiply_convert_fusion.3 = bf16[4,512,2048]{2,1,0:T(8,128)(2,1)} fusion(f32[4,512,2048]{2,1,0:T(8,128)} %get-tuple-element.553, f32[4,512,2048]{2,1,0:T(8,128)S(1)} %fusion.154, f32[4,512]{1,0:T(4,128)S(1)} %get-tuple-element.554, f32[4,512]{1,0:T(4,128)S(1)} %dynamic-slice_bitcast_fusion.2, pred[2048]{0:T(1024)(128)(4,1)S(1)} %convert_compare_fusion.5), kind=kLoop, calls=%fused_computation.24.clone.1 | loop fusion | flops 25165824 | bytes 41961472 | tf_op jit(solution)/shard_map/while/body/eval_jaxpr/while/body/eval_jaxpr/convert_element_type | solution.py:88
  410.2 6.9 fusion.157
  431.9 9.5 %multiply_reduce_fusion.8 = (f32[4,512]{1,0:T(4,128)S(1)}, f32[4,512,2048]{2,1,0:T(8,128)}) fusion(f32[4,512,2048]{2,1,0:T(8,128)S(1)} %fusion.154, f32[4,512]{1,0:T(4,128)S(1)} %dynamic-slice_bitcast_fusion.2, pred[2048]{0:T(1024)(128)(4,1)S(1)} %convert_compare_fusion.5, bf16[2048,4,64]{0,2,1:T(8,128)(2,1)S(1)} %get-tuple-element.611, ...), kind=kOutput, calls=%fused_computation.25.clone.1 | convolution fusion | flops 557840384 | bytes 34883588 | tf_op jit(solution)/shard_map/while/body/eval_jaxpr/while/body/eval_jaxpr/qhk,shk->hqs/dot_general | solution.py:84
  441.4 10.7 %multiply_convert_fusion.3 = bf16[4,512,2048]{2,1,0:T(8,128)(2,1)} fusion(f32[4,512,2048]{2,1,0:T(8,128)} %get-tuple-element.553, f32[4,512,2048]{2,1,0:T(8,128)S(1)} %fusion.154, f32[4,512]{1,0:T(4,128)S(1)} %get-tuple-element.554, f32[4,512]{1,0:T(4,128)S(1)} %dynamic-slice_bitcast_fusion.2, pred[2048]{0:T(1024)(128)(4,1)S(1)} %convert_compare_fusion.5), kind=kLoop, calls=%fused_computation.24.clone.1 | loop fusion | flops 25165824 | bytes 41961472 | tf_op jit(solution)/shard_map/while/body/eval_jaxpr/while/body/eval_jaxpr/convert_element_type | solution.py:88
  452.1 6.9 fusion.157
  490.6 17.5 %scatter_custom_fusion = f32[12800,256]{1,0:T(8,128)} fusion(s32[2048]{0:T(1024)S(1)} %bitcast.187, f32[2048,256]{1,0:T(8,128)} %copy.90, f32[]{:T(128)} %constant.51.clone.1), kind=kCustom, calls=%fused_computation.57 | custom fusion | flops 524288 | bytes 13107712 | tf_op jit(solution)/shard_map/scatter-add | solution.py:281
  513.3 26.0 %reduce-scatter.15.cloned.1.call-done = f32[512,256]{0,1:T(8,128)} async-done(((f32[2048,256]{0,1:T(8,128)}), f32[512,256]{0,1:T(8,128)}) %reduce-scatter.15.cloned.1.call-update) | async-done | bytes 524304 | tf_op jit(solution)/shard_map/reduce_scatter | solution.py:307
  539.2 222.0 %reduce-scatter.9.cloned.1.call-done = f32[3200,256]{1,0:T(8,128)} async-done(((f32[12800,256]{1,0:T(8,128)}), f32[3200,256]{1,0:T(8,128)}) %reduce-scatter.9.cloned.1.call-update) | async-done | bytes 3276816 | tf_op jit(solution)/shard_map/reduce_scatter | solution.py:303
  761.3 11.3 %scatter_custom_fusion.1 = f32[12800]{0:T(1024)S(1)} fusion(s32[2048]{0:T(1024)S(1)} %bitcast.188, f32[2048]{0:T(1024)S(1)} %copy-done.36, f32[]{:T(128)} %constant.51.clone.1), kind=kCustom, calls=%fused_computation.126 | custom fusion | flops 2048 | bytes 51204 | tf_op jit(solution)/shard_map/scatter-add | solution.py:282
  780.6 19.4 %all-reduce.20 = (f32[12800]{0:T(1024)S(1)}, f32[256]{0:T(256)S(1)}, f32[256]{0:T(256)S(1)}, f32[256]{0:T(256)S(1)}, f32[256]{0:T(256)S(1)}, /*index=5*/f32[256]...) all-reduce(f32[12800]{0:T(1024)S(1)} %scatter_custom_fusion.1, ...), channel_id=3, replica_groups=mesh['dp'=8,'fsdp'=4] {'fsdp'}, use_global_device_ids=true, to_apply=%region_19.20.clone | all-reduce | flops 15360 | bytes 122880
  804.2 25.4 %all-reduce.18 = (f32[3200]{0:T(1024)S(1)}, f32[16,256]{1,0:T(8,128)}, f32[16,256]{1,0:T(8,128)}, f32[64]{0:T(128)}, f32[64]{0:T(128)}, /*index=5*/f32[64]{0:T(1...) all-reduce(f32[3200]{0:T(1024)S(1)} %dynamic-slice.14, ...), channel_id=1, replica_groups=mesh['dp'=8,'fsdp'=4] {'dp'}, use_global_device_ids=true, to_apply=%region_20.21 | all-reduce | flops 12032 | bytes 96256 | tf_op jit(solution)/shard_map/psum | solution.py:341
  830.2 60.0 %all-reduce.24.cloned.1.call-done = (f32[3200,256]{1,0:T(8,128)}, f32[512,256]{0,1:T(8,128)}, f32[64,768]{1,0:T(8,128)}, f32[64,256]{1,0:T(8,128)}, f32[64,512]{1,0:T(8,128)}, /*index=5*/f32[128,256]{1,0:T(8,128)}) async-done(((f32[3200,256]{1,0:T(8,128)}, f32[512,256]{0,1:T(8,128)}, f32[64,768]{1,0:T(8,128)}, f32[64,256]{1,0:T(8,128)}, f32[64,512]{1,0:T(8,128)}, /*index=5*/f32[128,256]{1,0:T(8,128)}), ...) | async-done | bytes 4325392 | tf_op jit(solution)/shard_map/psum | solution.py:341
  (332 shorter events, 234.4 us)
Async XLA Ops:
  7.2 160.6 %all-gather.4.cloned.1.call-start = ((), (), s32[]{:S(2)}) async-start(), calls=%async_computation.8 | async-start | bytes 8192000 | tf_op jit(solution)/shard_map/all_gather | solution.py:156
  7.9 173.8 %all-gather.6.cloned.1.call-start = ((), (), s32[]{:S(2)}) async-start(), calls=%async_computation.9 | async-start | bytes 1310720 | tf_op jit(solution)/shard_map/all_gather | solution.py:159
  9.8 503.4 %reduce-scatter.19.cloned.1.call-start = ((), (), s32[]{:S(2)}) async-start(), calls=%async_computation.15 | async-start | bytes 327680 | tf_op jit(solution)/shard_map/reduce_scatter | solution.py:313
  65.2 8.2 copy-start.27
  72.7 19.5 %copy-start.49 = (bf16[64,256]{1,0:T(8,128)(2,1)S(1)}, bf16[64,256]{1,0:T(8,128)(2,1)}, u32[]{:S(2)}) copy-start(bf16[64,256]{1,0:T(8,128)(2,1)} %param.42) | copy-start | bytes 98308
  72.7 38.4 %copy-start.44 = (bf16[64,512]{1,0:T(8,128)(2,1)S(1)}, bf16[64,512]{1,0:T(8,128)(2,1)}, u32[]{:S(2)}) copy-start(bf16[64,512]{1,0:T(8,128)(2,1)} %param.46) | copy-start | bytes 196612
  72.7 60.5 %copy-start.45 = (bf16[128,256]{1,0:T(8,128)(2,1)S(1)}, bf16[128,256]{1,0:T(8,128)(2,1)}, u32[]{:S(2)}) copy-start(bf16[128,256]{1,0:T(8,128)(2,1)} %param.48) | copy-start | bytes 196612
  73.4 94.4 %copy-start.50 = (s32[1,2048]{1,0:T(1,128)S(1)}, s32[1,2048]{1,0:T(1,128)}, u32[]{:S(2)}) copy-start(s32[1,2048]{1,0:T(1,128)} %param.27) | copy-start | bytes 24580
  150.7 31.0 %copy-start.34 = (f32[2048]{0:T(1024)}, f32[2048]{0:T(1024)S(1)}, u32[]{:S(2)}) copy-start(f32[2048]{0:T(1024)S(1)} %fusion.78) | copy-start | bytes 24580
  167.8 16.4 %copy-start.20 = (bf16[256,768]{1,0:T(8,128)(2,1)}, bf16[256,768]{1,0:T(8,128)(2,1)S(1)}, u32[]{:S(2)}) copy-start(bf16[256,768]{1,0:T(8,128)(2,1)S(1)} %all_gather.63) | copy-start | bytes 1179652
  167.8 13.9 %copy-start.63 = (f32[1,256]{1,0:T(1,128)S(1)}, f32[1,256]{1,0:T(1,128)}, u32[]{:S(2)}) copy-start(f32[1,256]{1,0:T(1,128)} %dynamic-slice_convert_fusion) | copy-start | bytes 3076
  248.9 11.5 %copy-start.4 = (f32[2048,256]{0,1:T(8,128)}, f32[2048,256]{0,1:T(8,128)S(1)}, u32[]{:S(2)}) copy-start(f32[2048,256]{0,1:T(8,128)S(1)} %get-tuple-element.435) | copy-start | bytes 6291460
  249.5 11.0 %copy-start.15 = (bf16[1,2048,256]{1,2,0:T(8,128)(2,1)S(1)}, bf16[1,2048,256]{1,2,0:T(8,128)(2,1)}, u32[]{:S(2)}) copy-start(bf16[1,2048,256]{1,2,0:T(8,128)(2,1)} %copy.83) | copy-start | bytes 3145732
  249.5 11.0 %copy-start.24 = (bf16[512,256]{1,0:T(8,128)(2,1)S(1)}, bf16[512,256]{1,0:T(8,128)(2,1)}, u32[]{:S(2)}) copy-start(bf16[512,256]{1,0:T(8,128)(2,1)} %all_gather.72) | copy-start | bytes 786436
  249.5 11.0 %copy-start.35 = (f32[2048]{0:T(1024)S(1)}, f32[2048]{0:T(1024)}, u32[]{:S(2)}) copy-start(f32[2048]{0:T(1024)} %copy-done.34) | copy-start | bytes 24580
  278.0 235.2 %reduce-scatter.21.cloned.1.call-start = ((), (), s32[]{:S(2)}) async-start(), calls=%async_computation.16 | async-start | bytes 655360 | tf_op jit(solution)/shard_map/reduce_scatter | solution.py:317
  281.9 231.4 %reduce-scatter.23.cloned.1.call-start = ((), (), s32[]{:S(2)}) async-start(), calls=%async_computation.17 | async-start | bytes 655360 | tf_op jit(solution)/shard_map/reduce_scatter | solution.py:319
  296.9 216.3 %reduce-scatter.17.cloned.1.call-start = ((), (), s32[]{:S(2)}) async-start(), calls=%async_computation.14 | async-start | bytes 983040 | tf_op jit(solution)/shard_map/reduce_scatter | solution.py:310
  327.1 6.9 copy-start
  368.3 6.9 copy-start
  410.2 6.9 copy-start
  452.1 6.9 copy-start
  472.8 66.5 %reduce-scatter.15.cloned.1.call-start = ((), (), s32[]{:S(2)}) async-start(), calls=%async_computation.13 | async-start | bytes 2621440 | tf_op jit(solution)/shard_map/reduce_scatter | solution.py:307
  487.2 274.0 %reduce-scatter.9.cloned.1.call-start = ((), (), s32[]{:S(2)}) async-start(), calls=%async_computation.10 | async-start | bytes 16384000 | tf_op jit(solution)/shard_map/reduce_scatter | solution.py:303
  508.1 292.7 %reduce-scatter.13.cloned.1.call-start = ((), (), s32[]{:S(2)}) async-start(), calls=%async_computation.12 | async-start | bytes 81920 | tf_op jit(solution)/shard_map/reduce_scatter | solution.py:306
  508.9 295.2 %reduce-scatter.11.cloned.1.call-start = ((), (), s32[]{:S(2)}) async-start(), calls=%async_computation.11 | async-start | bytes 81920 | tf_op jit(solution)/shard_map/reduce_scatter | solution.py:305
  509.2 265.3 %copy-start.71 = (bf16[256]{0:T(256)(128)(2,1)S(1)}, bf16[256]{0:T(256)(128)(2,1)}, u32[]{:S(2)}) copy-start(bf16[256]{0:T(256)(128)(2,1)} %get-tuple-element.412) | copy-start | bytes 1540
  509.2 265.3 %copy-start.6 = (f32[2048,256]{0,1:T(8,128)S(1)}, f32[2048,256]{0,1:T(8,128)}, u32[]{:S(2)}) copy-start(f32[2048,256]{0,1:T(8,128)} %copy-done.4) | copy-start | bytes 6291460
  509.2 265.3 %copy-start.25 = (bf16[512,256]{1,0:T(8,128)(2,1)S(1)}, bf16[512,256]{1,0:T(8,128)(2,1)}, u32[]{:S(2)}) copy-start(bf16[512,256]{1,0:T(8,128)(2,1)} %all_gather.72) | copy-start | bytes 786436
  513.1 377.1 %all-reduce.24.cloned.1.call-start = ((), (), s32[]{:S(2)}) async-start(), calls=%async_computation.18 | async-start | bytes 8650752 | tf_op jit(solution)/shard_map/psum | solution.py:341
  774.5 6.1 copy-start.57
  774.5 6.1 copy-start.60
  (55 other events, 160.1 us)
Sparse Core Ops, SparseCore 0:
  9.6 133.5 all-gather.3
  145.3 29.6 all-gather.5
  278.1 16.6 reduce-scatter.18
  297.6 19.8 reduce-scatter.20
  319.8 19.8 reduce-scatter.22
  472.9 20.1 reduce-scatter.16
  496.1 43.1 reduce-scatter.14
  541.6 219.6 reduce-scatter.8
  764.1 20.0 reduce-scatter.12
  786.9 17.1 reduce-scatter.10
  808.0 82.1 all-reduce.23
where the time goes:
time: 911 us; the launch traced here: 906 us
  waiting for transfers between devices  312 us (34%)
  matrix products  201 us (22%)
  blocking collectives  176 us (19%)
  other arithmetic  119 us (13%)
  local copies, waits for them, and re-layouts  77.5 us (9%)
  between operations  19.1 us (2%)
    reduce_scatter x1, waiting for transfers between devices, body(): lax.psum_scatter(dense_grad, 'fsdp', scatter_dimension=0, tiled=True)  222 us
    psum x1, waiting for transfers between devices, body(): lax.psum((table_share, count_share, expr_share, study_share, position_sha...  60 us
    convert_element_type x4, other arithmetic, one_block(): grad_scores = (probs * (grad_probs - inner)).astype(jnp.bfloat16)  42.7 us
    dot_general x4, matrix products, one_block(): jnp.einsum('qhk,shk->hqs', grad_block, values, preferred_element_type=jnp...  38.1 us
    unnamed x185, local copies, waits for them, and re-layouts  37.2 us
    unnamed x2, blocking collectives  35.6 us
    dot_general x4, matrix products, one_block(): jnp.einsum('hqs,shk->qhk', grad_scores, keys, preferred_element_type=jnp....  27.6 us
    dot_general x8, matrix products, one_block(): jnp.einsum('qhk,shk->hqs', query_block, keys, preferred_element_type=jnp....  27.3 us
  transfers between devices with their start and end apart: 11, of which 4 were waited for; matrix products, arithmetic and copies ran while one was open for 32% of the time, Pallas kernels for 0%

commit v1 on v0

--- a/solution.py
+++ b/solution.py
@@ -6,6 +6,29 @@
 HEADS = 4
 epsilon = 1e-05
 highest = lax.Precision.HIGHEST
+
+
+def in_order(blocks, dim):
+    dims = list(blocks.shape[1:])
+    dims[dim] *= blocks.shape[0]
+    return jnp.moveaxis(blocks, 0, dim).reshape(dims)
+
+
+def collected_by_bits(x, axis):
+    size, here = (lax.axis_size(axis), lax.axis_index(axis))
+    blocks, bit = (x[None], 1)
+    while bit < size:
+        partner_block = lax.ppermute(blocks, axis, [(i, i ^ bit) for i in range(size)])
+        low = here & bit == 0
+        blocks = jnp.concatenate(
+            [jnp.where(low, blocks, partner_block), jnp.where(low, partner_block, blocks)]
+        )
+        bit *= 2
+    return blocks
+
+
+def doubled_up(x, axis, dim):
+    return in_order(collected_by_bits(x, axis), dim)
 
 
 def normalize(values):
@@ -162,7 +185,7 @@
         lax.all_gather(w_qkv, "fsdp", axis=0, tiled=True),
         lax.all_gather(bias_query, "fsdp", axis=0, tiled=True),
         lax.all_gather(bias_value, "fsdp", axis=0, tiled=True),
-        lax.all_gather(w_output, "fsdp", axis=0, tiled=True),
+        doubled_up(w_output, "fsdp", 0),
         lax.all_gather(bias_output, "fsdp", axis=0, tiled=True),
         lax.all_gather(norm2_gain, "fsdp", axis=0, tiled=True),
         lax.all_gather(norm2_shift, "fsdp", axis=0, tiled=True),

time: 911 us -> 925 us (1.015)
  waiting for transfers between devices: 312 us -> 327 us
    all_gather x1, waiting for transfers between devices: 0.02 us -> 12.7 us  [body(): lax.all_gather(position_table, 'fsdp', axis=0, tiled=True)]
    unnamed x185 -> x197, local copies, waits for them, and re-layouts: 37.2 us -> 31.5 us
  transfers between devices with their start and end apart: 11 -> 13, of which waited for: 4 -> 5; matrix products, arithmetic and copies ran while one was open for 32% -> 31% of each run, Pallas kernels for 0% -> 0%
where the time goes in v1:
time: 925 us; the launch traced here: 919 us
  waiting for transfers between devices  327 us (35%)
  matrix products  201 us (22%)
  blocking collectives  172 us (19%)
  other arithmetic  122 us (13%)
  local copies, waits for them, and re-layouts  71.9 us (8%)
  between operations  19.1 us (2%)
    reduce_scatter x1, waiting for transfers between devices, body(): lax.psum_scatter(dense_grad, 'fsdp', scatter_dimension=0, tiled=True)  222 us
    psum x1, waiting for transfers between devices, body(): lax.psum((table_share, count_share, expr_share, study_share, position_sha...  60.2 us
    convert_element_type x4, other arithmetic, one_block(): grad_scores = (probs * (grad_probs - inner)).astype(jnp.bfloat16)  42.9 us
    dot_general x4, matrix products, one_block(): jnp.einsum('qhk,shk->hqs', grad_block, values, preferred_element_type=jnp...  38 us
    unnamed x197, local copies, waits for them, and re-layouts  31.5 us
    unnamed x2, blocking collectives  29.2 us
    reduce_scatter x1, waiting for transfers between devices, body(): lax.psum_scatter(grad_position, 'fsdp', scatter_dimension=0, tiled=True)  28.3 us
    dot_general x4, matrix products, one_block(): jnp.einsum('hqs,shk->qhk', grad_scores, keys, preferred_element_type=jnp....  27.6 us
  transfers between devices with their start and end apart: 13, of which 5 were waited for; matrix products, arithmetic and copies ran while one was open for 31% of the time, Pallas kernels for 0%

profile of v1, /device:TPU:0, one launch (start us, length us, event | category | flops | bytes accessed | tf_op | source)
XLA Modules:
  0.0 918.7 jit_solution(10447657815320737999)
XLA Ops:
  15.1 13.7 %all_gather.58 = bf16[64,256]{1,0:T(8,128)(2,1)S(1)} all-gather(bf16[16,256]{1,0:T(8,128)(2,1)} %param.35), channel_id=1, replica_groups=mesh['dp'=8,'fsdp'=4] {'fsdp'}, dimensions={0}, use_global_device_ids=true | all-gather | bytes 40960 | tf_op jit(solution)/shard_map/all_gather | solution.py:181
  28.8 21.9 %all_gather.62 = bf16[256,768]{1,0:T(8,128)(2,1)S(1)} all-gather(bf16[64,768]{1,0:T(8,128)(2,1)} %param.39), channel_id=1, replica_groups=mesh['dp'=8,'fsdp'=4] {'fsdp'}, dimensions={0}, use_global_device_ids=true | all-gather | bytes 491520 | tf_op jit(solution)/shard_map/all_gather | solution.py:185
  52.0 20.5 %all_gather.68 = bf16[256,512]{1,0:T(8,128)(2,1)} all-gather(bf16[64,512]{1,0:T(8,128)(2,1)} %param.46), channel_id=1, replica_groups=mesh['dp'=8,'fsdp'=4] {'fsdp'}, dimensions={0}, use_global_device_ids=true | all-gather | bytes 327680 | tf_op jit(solution)/shard_map/all_gather | solution.py:192
  75.7 9.8 %all-reduce.21 = (bf16[256]{0:T(256)(128)(2,1)S(1)}, bf16[256]{0:T(256)(128)(2,1)S(1)}, bf16[256]{0:T(256)(128)(2,1)S(1)}, bf16[256]{0:T(256)(128)(2,1)S(1)}, bf...) all-reduce(bf16[256]{0:T(256)(128)(2,1)S(1)} %dynamic-update-slice., ...), channel_id=1, replica_groups=mesh['dp'=8,'fsdp'=4] {'fsdp'}, use_global_device_ids=true, to_apply=%add.1 | all-reduce | flops 2048 | bytes 8192
  89.4 12.9 %all-gather = bf16[4,1,128]{2,1,0:T(2,128)(2,1)S(1)} all-gather(bf16[1,1,128]{2,1,0:T(2,128)(2,1)S(1)} %bitcast.198), channel_id=1, replica_groups=mesh['dp'=8,'fsdp'=4] {'fsdp'}, dimensions={0}, use_global_device_ids=true | all-gather | bytes 1280 | tf_op jit(solution)/shard_map/all_gather | solution.py:193
  102.9 16.0 %all_gather.57 = bf16[64,256]{1,0:T(8,128)(2,1)S(1)} all-gather(bf16[16,256]{1,0:T(8,128)(2,1)S(1)} %copy-done.52), channel_id=1, replica_groups=mesh['dp'=8,'fsdp'=4] {'fsdp'}, dimensions={0}, use_global_device_ids=true | all-gather | bytes 40960 | tf_op jit(solution)/shard_map/all_gather | solution.py:180
  118.9 7.5 gather_fusion.1
  132.7 18.5 %all_gather.70 = bf16[512,256]{1,0:T(8,128)(2,1)} all-gather(bf16[128,256]{1,0:T(8,128)(2,1)} %param.48), channel_id=1, replica_groups=mesh['dp'=8,'fsdp'=4] {'fsdp'}, dimensions={0}, use_global_device_ids=true | all-gather | bytes 327680 | tf_op jit(solution)/shard_map/all_gather | solution.py:194
  151.9 12.2 %gather_fusion = bf16[2048,256]{1,0:T(8,128)(2,1)} fusion(bf16[12800,256]{1,0:T(8,128)(2,1)} %all-gather.4.cloned.1.call-done, s32[2048]{0:T(1024)S(1)} %broadcast_clamp_fusion.1), kind=kCustom, calls=%fused_computation | custom fusion | bytes 2105344 | tf_op jit(solution)/shard_map/gather | solution.py:212
  165.6 12.7 %all-gather.6.cloned.1.call-done = bf16[2048,256]{0,1:T(8,128)(2,1)} async-done(((bf16[512,256]{0,1:T(8,128)(2,1)}), bf16[2048,256]{0,1:T(8,128)(2,1)}) %all-gather.6.cloned.1.call-update) | async-done | bytes 1048592 | tf_op jit(solution)/shard_map/all_gather | solution.py:182
  188.5 53.9 %while.49 = (s32[]{:T(128)}, bf16[4,512,4,64]{1,3,2,0:T(8,128)(2,1)}, f32[4,4,512]{2,1,0:T(4,128)S(1)}, bf16[4,512,4,64]{1,3,2,0:T(8,128)(2,1)}, bf16[2048,4,64]...) while((s32[]{:T(128)}, bf16[4,512,4,64]{1,3,2,0:T(8,128)(2,1)}, ...), condition=%wide.region_5.6_spmd.clone, body=%wide.region_2.5_spmd.clone.sunk | while | flops 1124208640 | bytes 53026924 | solution.py:87
  246.1 10.9 %multiply_convert_fusion.1 = (bf16[2048,512]{1,0:T(8,128)(2,1)}, f32[2048,512]{1,0:T(8,128)S(1)}, f32[2048,512]{1,0:T(8,128)S(1)}) fusion(f32[512]{0:T(512)S(1)} %bitcast.196, bf16[256,512]{1,0:T(8,128)(2,1)S(1)} %copy-done.25, f32[2048,256]{0,1:T(8,128)S(1)} %get-tuple-element.439, f32[256]{0:T(256)S(1)} %copy-done.78, f32[256]{0:T(256)S(1)} %copy-done.60, ...), kind=kOutput, calls=%fused_computation.63 | convolution fusion | flops 608698368 | bytes 12865536 | tf_op jit(solution)/shard_map/dot_general | solution.py:48
  278.6 14.0 %all_gather.72 = bf16[256,256]{1,0:T(8,128)(2,1)S(1)} all-gather(bf16[64,256]{1,0:T(8,128)(2,1)S(1)} %copy-done.40), channel_id=1, replica_groups=mesh['dp'=8,'fsdp'=4] {'fsdp'}, dimensions={0}, use_global_device_ids=true | all-gather | bytes 163840 | tf_op jit(solution)/shard_map/all_gather | solution.py:245
  307.6 166.9 %while.50 = (s32[]{:T(128)}, f32[2048,4,64]{0,2,1:T(8,128)}, f32[2048,4,64]{0,2,1:T(8,128)}, bf16[4,512,4,64]{1,3,2,0:T(8,128)(2,1)}, bf16[4,512,4,64]{1,3,2,0:T...) while((s32[]{:T(128)}, f32[2048,4,64]{0,2,1:T(8,128)}, ...), condition=%wide.region_12.13_spmd.clone, body=%wide.region_10.12_spmd.clone.sunk | while | flops 2750025728 | bytes 172556464 | solution.py:129
  317.4 9.5 %multiply_reduce_fusion.8 = (f32[4,512]{1,0:T(4,128)S(1)}, f32[4,512,2048]{2,1,0:T(8,128)}) fusion(f32[4,512,2048]{2,1,0:T(8,128)S(1)} %fusion.154, f32[4,512]{1,0:T(4,128)S(1)} %dynamic-slice_bitcast_fusion.2, pred[2048]{0:T(1024)(128)(4,1)S(1)} %convert_compare_fusion.5, bf16[2048,4,64]{0,2,1:T(8,128)(2,1)S(1)} %get-tuple-element.615, ...), kind=kOutput, calls=%fused_computation.25.clone.1 | convolution fusion | flops 557840384 | bytes 34883588 | tf_op jit(solution)/shard_map/while/body/eval_jaxpr/while/body/eval_jaxpr/qhk,shk->hqs/dot_general | solution.py:107
  326.9 10.7 %multiply_convert_fusion.3 = bf16[4,512,2048]{2,1,0:T(8,128)(2,1)} fusion(f32[4,512,2048]{2,1,0:T(8,128)} %get-tuple-element.557, f32[4,512,2048]{2,1,0:T(8,128)S(1)} %fusion.154, f32[4,512]{1,0:T(4,128)S(1)} %get-tuple-element.558, f32[4,512]{1,0:T(4,128)S(1)} %dynamic-slice_bitcast_fusion.2, pred[2048]{0:T(1024)(128)(4,1)S(1)} %convert_compare_fusion.5), kind=kLoop, calls=%fused_computation.24.clone.1 | loop fusion | flops 25165824 | bytes 41961472 | tf_op jit(solution)/shard_map/while/body/eval_jaxpr/while/body/eval_jaxpr/convert_element_type | solution.py:111
  337.7 6.9 fusion.157
  358.7 9.5 %multiply_reduce_fusion.8 = (f32[4,512]{1,0:T(4,128)S(1)}, f32[4,512,2048]{2,1,0:T(8,128)}) fusion(f32[4,512,2048]{2,1,0:T(8,128)S(1)} %fusion.154, f32[4,512]{1,0:T(4,128)S(1)} %dynamic-slice_bitcast_fusion.2, pred[2048]{0:T(1024)(128)(4,1)S(1)} %convert_compare_fusion.5, bf16[2048,4,64]{0,2,1:T(8,128)(2,1)S(1)} %get-tuple-element.615, ...), kind=kOutput, calls=%fused_computation.25.clone.1 | convolution fusion | flops 557840384 | bytes 34883588 | tf_op jit(solution)/shard_map/while/body/eval_jaxpr/while/body/eval_jaxpr/qhk,shk->hqs/dot_general | solution.py:107
  368.2 10.7 %multiply_convert_fusion.3 = bf16[4,512,2048]{2,1,0:T(8,128)(2,1)} fusion(f32[4,512,2048]{2,1,0:T(8,128)} %get-tuple-element.557, f32[4,512,2048]{2,1,0:T(8,128)S(1)} %fusion.154, f32[4,512]{1,0:T(4,128)S(1)} %get-tuple-element.558, f32[4,512]{1,0:T(4,128)S(1)} %dynamic-slice_bitcast_fusion.2, pred[2048]{0:T(1024)(128)(4,1)S(1)} %convert_compare_fusion.5), kind=kLoop, calls=%fused_computation.24.clone.1 | loop fusion | flops 25165824 | bytes 41961472 | tf_op jit(solution)/shard_map/while/body/eval_jaxpr/while/body/eval_jaxpr/convert_element_type | solution.py:111
  378.9 6.9 fusion.157
  400.6 9.5 %multiply_reduce_fusion.8 = (f32[4,512]{1,0:T(4,128)S(1)}, f32[4,512,2048]{2,1,0:T(8,128)}) fusion(f32[4,512,2048]{2,1,0:T(8,128)S(1)} %fusion.154, f32[4,512]{1,0:T(4,128)S(1)} %dynamic-slice_bitcast_fusion.2, pred[2048]{0:T(1024)(128)(4,1)S(1)} %convert_compare_fusion.5, bf16[2048,4,64]{0,2,1:T(8,128)(2,1)S(1)} %get-tuple-element.615, ...), kind=kOutput, calls=%fused_computation.25.clone.1 | convolution fusion | flops 557840384 | bytes 34883588 | tf_op jit(solution)/shard_map/while/body/eval_jaxpr/while/body/eval_jaxpr/qhk,shk->hqs/dot_general | solution.py:107
  410.1 10.7 %multiply_convert_fusion.3 = bf16[4,512,2048]{2,1,0:T(8,128)(2,1)} fusion(f32[4,512,2048]{2,1,0:T(8,128)} %get-tuple-element.557, f32[4,512,2048]{2,1,0:T(8,128)S(1)} %fusion.154, f32[4,512]{1,0:T(4,128)S(1)} %get-tuple-element.558, f32[4,512]{1,0:T(4,128)S(1)} %dynamic-slice_bitcast_fusion.2, pred[2048]{0:T(1024)(128)(4,1)S(1)} %convert_compare_fusion.5), kind=kLoop, calls=%fused_computation.24.clone.1 | loop fusion | flops 25165824 | bytes 41961472 | tf_op jit(solution)/shard_map/while/body/eval_jaxpr/while/body/eval_jaxpr/convert_element_type | solution.py:111
  420.9 6.9 fusion.157
  442.6 9.5 %multiply_reduce_fusion.8 = (f32[4,512]{1,0:T(4,128)S(1)}, f32[4,512,2048]{2,1,0:T(8,128)}) fusion(f32[4,512,2048]{2,1,0:T(8,128)S(1)} %fusion.154, f32[4,512]{1,0:T(4,128)S(1)} %dynamic-slice_bitcast_fusion.2, pred[2048]{0:T(1024)(128)(4,1)S(1)} %convert_compare_fusion.5, bf16[2048,4,64]{0,2,1:T(8,128)(2,1)S(1)} %get-tuple-element.615, ...), kind=kOutput, calls=%fused_computation.25.clone.1 | convolution fusion | flops 557840384 | bytes 34883588 | tf_op jit(solution)/shard_map/while/body/eval_jaxpr/while/body/eval_jaxpr/qhk,shk->hqs/dot_general | solution.py:107
  452.1 10.7 %multiply_convert_fusion.3 = bf16[4,512,2048]{2,1,0:T(8,128)(2,1)} fusion(f32[4,512,2048]{2,1,0:T(8,128)} %get-tuple-element.557, f32[4,512,2048]{2,1,0:T(8,128)S(1)} %fusion.154, f32[4,512]{1,0:T(4,128)S(1)} %get-tuple-element.558, f32[4,512]{1,0:T(4,128)S(1)} %dynamic-slice_bitcast_fusion.2, pred[2048]{0:T(1024)(128)(4,1)S(1)} %convert_compare_fusion.5), kind=kLoop, calls=%fused_computation.24.clone.1 | loop fusion | flops 25165824 | bytes 41961472 | tf_op jit(solution)/shard_map/while/body/eval_jaxpr/while/body/eval_jaxpr/convert_element_type | solution.py:111
  501.4 17.5 %scatter_custom_fusion = f32[12800,256]{1,0:T(8,128)} fusion(s32[2048]{0:T(1024)S(1)} %bitcast.193, f32[2048,256]{1,0:T(8,128)} %copy.90, f32[]{:T(128)} %constant.50.clone.1), kind=kCustom, calls=%fused_computation.57 | custom fusion | flops 524288 | bytes 13107712 | tf_op jit(solution)/shard_map/scatter-add | solution.py:304
  524.1 28.3 %reduce-scatter.15.cloned.1.call-done = f32[512,256]{0,1:T(8,128)} async-done(((f32[2048,256]{0,1:T(8,128)}), f32[512,256]{0,1:T(8,128)}) %reduce-scatter.15.cloned.1.call-update) | async-done | bytes 524304 | tf_op jit(solution)/shard_map/reduce_scatter | solution.py:330
  552.3 222.0 %reduce-scatter.9.cloned.1.call-done = f32[3200,256]{1,0:T(8,128)} async-done(((f32[12800,256]{1,0:T(8,128)}), f32[3200,256]{1,0:T(8,128)}) %reduce-scatter.9.cloned.1.call-update) | async-done | bytes 3276816 | tf_op jit(solution)/shard_map/reduce_scatter | solution.py:326
  774.4 11.3 %scatter_custom_fusion.1 = f32[12800]{0:T(1024)S(1)} fusion(s32[2048]{0:T(1024)S(1)} %bitcast.194, f32[2048]{0:T(1024)S(1)} %copy-done.36, f32[]{:T(128)} %constant.50.clone.1), kind=kCustom, calls=%fused_computation.132 | custom fusion | flops 2048 | bytes 51204 | tf_op jit(solution)/shard_map/scatter-add | solution.py:305
  793.7 19.4 %all-reduce.20 = (f32[12800]{0:T(1024)S(1)}, f32[256]{0:T(256)S(1)}, f32[256]{0:T(256)S(1)}, f32[256]{0:T(256)S(1)}, f32[256]{0:T(256)S(1)}, /*index=5*/f32[256]...) all-reduce(f32[12800]{0:T(1024)S(1)} %scatter_custom_fusion.1, ...), channel_id=3, replica_groups=mesh['dp'=8,'fsdp'=4] {'fsdp'}, use_global_device_ids=true, to_apply=%region_19.20.clone | all-reduce | flops 15360 | bytes 122880
  817.2 25.4 %all-reduce.18 = (f32[3200]{0:T(1024)S(1)}, f32[16,256]{1,0:T(8,128)}, f32[16,256]{1,0:T(8,128)}, f32[64]{0:T(128)}, f32[64]{0:T(128)}, /*index=5*/f32[64]{0:T(1...) all-reduce(f32[3200]{0:T(1024)S(1)} %dynamic-slice.14, ...), channel_id=1, replica_groups=mesh['dp'=8,'fsdp'=4] {'dp'}, use_global_device_ids=true, to_apply=%region_20.21 | all-reduce | flops 12032 | bytes 96256 | tf_op jit(solution)/shard_map/psum | solution.py:364
  843.2 60.2 %all-reduce.24.cloned.1.call-done = (f32[3200,256]{1,0:T(8,128)}, f32[512,256]{0,1:T(8,128)}, f32[64,768]{1,0:T(8,128)}, f32[64,256]{1,0:T(8,128)}, f32[64,512]{1,0:T(8,128)}, /*index=5*/f32[128,256]{1,0:T(8,128)}) async-done(((f32[3200,256]{1,0:T(8,128)}, f32[512,256]{0,1:T(8,128)}, f32[64,768]{1,0:T(8,128)}, f32[64,256]{1,0:T(8,128)}, f32[64,512]{1,0:T(8,128)}, /*index=5*/f32[128,256]{1,0:T(8,128)}), ...) | async-done | bytes 4325392 | tf_op jit(solution)/shard_map/psum | solution.py:364
  (352 shorter events, 243.0 us)
Async XLA Ops:
  7.2 65.3 %copy-start.62 = (u32[32]{0:T(128)S(1)}, u32[32]{0:T(128)}, u32[]{:S(2)}) copy-start(u32[32]{0:T(128)} %constant.209) | copy-start | bytes 388
  7.2 66.5 %copy-start.69 = (bf16[64]{0:T(256)(128)(2,1)S(1)}, bf16[64]{0:T(256)(128)(2,1)}, u32[]{:S(2)}) copy-start(bf16[64]{0:T(256)(128)(2,1)} %param.44) | copy-start | bytes 388
  7.2 66.8 %copy-start.70 = (bf16[64]{0:T(256)(128)(2,1)S(1)}, bf16[64]{0:T(256)(128)(2,1)}, u32[]{:S(2)}) copy-start(bf16[64]{0:T(256)(128)(2,1)} %param.45) | copy-start | bytes 388
  7.2 67.0 %copy-start.71 = (bf16[64]{0:T(256)(128)(2,1)S(1)}, bf16[64]{0:T(256)(128)(2,1)}, u32[]{:S(2)}) copy-start(bf16[64]{0:T(256)(128)(2,1)} %param.43) | copy-start | bytes 388
  7.2 67.3 %copy-start.72 = (bf16[64]{0:T(256)(128)(2,1)S(1)}, bf16[64]{0:T(256)(128)(2,1)}, u32[]{:S(2)}) copy-start(bf16[64]{0:T(256)(128)(2,1)} %param.41) | copy-start | bytes 388
  7.2 67.5 %copy-start.73 = (bf16[64]{0:T(256)(128)(2,1)S(1)}, bf16[64]{0:T(256)(128)(2,1)}, u32[]{:S(2)}) copy-start(bf16[64]{0:T(256)(128)(2,1)} %param.40) | copy-start | bytes 388
  7.3 67.7 %copy-start.74 = (bf16[64]{0:T(256)(128)(2,1)S(1)}, bf16[64]{0:T(256)(128)(2,1)}, u32[]{:S(2)}) copy-start(bf16[64]{0:T(256)(128)(2,1)} %param.37) | copy-start | bytes 388
  7.3 68.0 %copy-start.75 = (bf16[64]{0:T(256)(128)(2,1)S(1)}, bf16[64]{0:T(256)(128)(2,1)}, u32[]{:S(2)}) copy-start(bf16[64]{0:T(256)(128)(2,1)} %param.38) | copy-start | bytes 388
  7.3 68.2 %copy-start.76 = (bf16[64]{0:T(256)(128)(2,1)S(1)}, bf16[64]{0:T(256)(128)(2,1)}, u32[]{:S(2)}) copy-start(bf16[64]{0:T(256)(128)(2,1)} %param.49) | copy-start | bytes 388
  7.3 82.1 %copy-start.68 = (bf16[128]{0:T(256)(128)(2,1)S(1)}, bf16[128]{0:T(256)(128)(2,1)}, u32[]{:S(2)}) copy-start(bf16[128]{0:T(256)(128)(2,1)} %param.47) | copy-start | bytes 772
  7.3 95.6 %copy-start.52 = (bf16[16,256]{1,0:T(8,128)(2,1)S(1)}, bf16[16,256]{1,0:T(8,128)(2,1)}, u32[]{:S(2)}) copy-start(bf16[16,256]{1,0:T(8,128)(2,1)} %param.34) | copy-start | bytes 24580
  7.3 144.6 %all-gather.4.cloned.1.call-start = ((), (), s32[]{:S(2)}) async-start(), calls=%async_computation.8 | async-start | bytes 8192000 | tf_op jit(solution)/shard_map/all_gather | solution.py:179
  8.0 170.3 %all-gather.6.cloned.1.call-start = ((), (), s32[]{:S(2)}) async-start(), calls=%async_computation.9 | async-start | bytes 1310720 | tf_op jit(solution)/shard_map/all_gather | solution.py:182
  8.1 121.9 %collective-permute-start = (bf16[1,64,256]{2,1,0:T(8,128)(2,1)}, bf16[1,64,256]{2,1,0:T(8,128)(2,1)}, u32[]{:S(2)}, u32[]{:S(2)}) collective-permute-start(bf16[1,64,256]{2,1,0:T(8,128)(2,1)} %bitcast.189), channel_id=1, source_target_pairs={{0,1},{1,0},{2,3},{3,2},{4,5},{5,4},{6,7},{7,6},{8,9},{9,8},{10,11... | collective-permute-start | bytes 98312 | tf_op jit(solution)/shard_map/ppermute | solution.py:21
  13.0 511.0 %reduce-scatter.19.cloned.1.call-start = ((), (), s32[]{:S(2)}) async-start(), calls=%async_computation.15 | async-start | bytes 327680 | tf_op jit(solution)/shard_map/reduce_scatter | solution.py:336
  14.4 164.0 %copy-start.34 = (f32[2048]{0:T(1024)}, f32[2048]{0:T(1024)S(1)}, u32[]{:S(2)}) copy-start(f32[2048]{0:T(1024)S(1)} %fusion.78) | copy-start | bytes 24580
  50.7 130.1 %copy-start.20 = (bf16[256,768]{1,0:T(8,128)(2,1)}, bf16[256,768]{1,0:T(8,128)(2,1)S(1)}, u32[]{:S(2)}) copy-start(bf16[256,768]{1,0:T(8,128)(2,1)S(1)} %all_gather.62) | copy-start | bytes 1179652
  130.8 20.4 %collective-permute-start.1 = (bf16[2,64,256]{2,1,0:T(8,128)(2,1)S(1)}, bf16[2,64,256]{2,1,0:T(8,128)(2,1)S(1)}, u32[]{:S(2)}, u32[]{:S(2)}) collective-permute-start(bf16[2,64,256]{2,1,0:T(8,128)(2,1)S(1)} %pad_maximum_fusion.4), channel_id=1, source_target_pairs={{0,2},{1,3},{2,0},{3,1},{4,6},{5,7},{6,4},{7,5},{8,10},{9,11},{10,... | collective-permute-start | bytes 196616 | tf_op jit(solution)/shard_map/ppermute | solution.py:21
  245.5 11.5 %copy-start.4 = (f32[2048,256]{0,1:T(8,128)}, f32[2048,256]{0,1:T(8,128)S(1)}, u32[]{:S(2)}) copy-start(f32[2048,256]{0,1:T(8,128)S(1)} %get-tuple-element.439) | copy-start | bytes 6291460
  246.0 10.9 %copy-start.15 = (bf16[1,2048,256]{1,2,0:T(8,128)(2,1)S(1)}, bf16[1,2048,256]{1,2,0:T(8,128)(2,1)}, u32[]{:S(2)}) copy-start(bf16[1,2048,256]{1,2,0:T(8,128)(2,1)} %copy.83) | copy-start | bytes 3145732
  246.0 10.9 %copy-start.23 = (bf16[512,256]{1,0:T(8,128)(2,1)S(1)}, bf16[512,256]{1,0:T(8,128)(2,1)}, u32[]{:S(2)}) copy-start(bf16[512,256]{1,0:T(8,128)(2,1)} %all_gather.70) | copy-start | bytes 786436
  274.6 249.4 %reduce-scatter.21.cloned.1.call-start = ((), (), s32[]{:S(2)}) async-start(), calls=%async_computation.16 | async-start | bytes 655360 | tf_op jit(solution)/shard_map/reduce_scatter | solution.py:340
  278.5 245.5 %reduce-scatter.23.cloned.1.call-start = ((), (), s32[]{:S(2)}) async-start(), calls=%async_computation.17 | async-start | bytes 655360 | tf_op jit(solution)/shard_map/reduce_scatter | solution.py:342
  307.5 216.5 %reduce-scatter.17.cloned.1.call-start = ((), (), s32[]{:S(2)}) async-start(), calls=%async_computation.14 | async-start | bytes 983040 | tf_op jit(solution)/shard_map/reduce_scatter | solution.py:333
  483.5 68.8 %reduce-scatter.15.cloned.1.call-start = ((), (), s32[]{:S(2)}) async-start(), calls=%async_computation.13 | async-start | bytes 2621440 | tf_op jit(solution)/shard_map/reduce_scatter | solution.py:330
  498.0 276.4 %reduce-scatter.9.cloned.1.call-start = ((), (), s32[]{:S(2)}) async-start(), calls=%async_computation.10 | async-start | bytes 16384000 | tf_op jit(solution)/shard_map/reduce_scatter | solution.py:326
  518.9 295.0 %reduce-scatter.13.cloned.1.call-start = ((), (), s32[]{:S(2)}) async-start(), calls=%async_computation.12 | async-start | bytes 81920 | tf_op jit(solution)/shard_map/reduce_scatter | solution.py:329
  519.7 297.5 %reduce-scatter.11.cloned.1.call-start = ((), (), s32[]{:S(2)}) async-start(), calls=%async_computation.11 | async-start | bytes 81920 | tf_op jit(solution)/shard_map/reduce_scatter | solution.py:328
  520.0 267.6 %copy-start.77 = (bf16[256]{0:T(256)(128)(2,1)S(1)}, bf16[256]{0:T(256)(128)(2,1)}, u32[]{:S(2)}) copy-start(bf16[256]{0:T(256)(128)(2,1)} %get-tuple-element.412) | copy-start | bytes 1540
  520.0 267.6 %copy-start.6 = (f32[2048,256]{0,1:T(8,128)S(1)}, f32[2048,256]{0,1:T(8,128)}, u32[]{:S(2)}) copy-start(f32[2048,256]{0,1:T(8,128)} %copy-done.4) | copy-start | bytes 6291460
  520.0 267.6 %copy-start.24 = (bf16[512,256]{1,0:T(8,128)(2,1)S(1)}, bf16[512,256]{1,0:T(8,128)(2,1)}, u32[]{:S(2)}) copy-start(bf16[512,256]{1,0:T(8,128)(2,1)} %all_gather.70) | copy-start | bytes 786436
  523.9 379.4 %all-reduce.24.cloned.1.call-start = ((), (), s32[]{:S(2)}) async-start(), calls=%async_computation.18 | async-start | bytes 8650752 | tf_op jit(solution)/shard_map/psum | solution.py:364
  (63 other events, 219.4 us)
Sparse Core Ops, SparseCore 0:
  9.7 140.0 all-gather.3
  151.9 26.3 all-gather.5
  274.8 19.6 reduce-scatter.18
  297.3 19.8 reduce-scatter.20
  319.4 19.9 reduce-scatter.22
  483.6 22.5 reduce-scatter.16
  509.2 43.1 reduce-scatter.14
  554.7 219.6 reduce-scatter.8
  777.2 19.9 reduce-scatter.12
  800.0 17.1 reduce-scatter.10
  821.0 82.2 all-reduce.23
